TPU v7x, 256 devices: a whole 4x4x8 slice. The times are simulated.
256 devices in a mesh: layer: 4 (over x), row: 8 (over y, core), col: 8 (over z).
Axes of the slice: x: 4, y: 4, z: 8, core: 2. Of those that a mesh axis runs over, the one named last changes fastest.
Arguments:
- left_values: bfloat16 [8192, 4, 2048], P('row', 'layer', 'col'), may hold values from -22 to 22
- left_pattern: int32 [32, 4, 8], P('row', 'layer', 'col'), may hold values from 0 to 1, as said below
- right_values: bfloat16 [8192, 4, 2048], P(('layer', 'row'), None, 'col'), may hold values from -6 to 6
- right_pattern: int32 [32, 4, 8], P(('layer', 'row'), None, 'col'), may hold values from 0 to 1, as said below
Outputs:
- expanded: bfloat16 [8192, 4, 2048], P('row', 'layer', 'col')
Inputs may be any that keep to these rules, and one draw needn't show every extreme that they name: `left_pattern`: 1 marks a stored tile, 0 an absent one. `right_pattern`: 1 marks a stored tile, 0 an absent one.
All inputs are finite; a program needn't handle non-finite values.
Results may differ from a plain program's by a relative error of at most 0.001.
Values may be sent and summed in bfloat16 or wider, within the bound.
A program may use at most 64 MiB of HBM per device.

v0:
```python
import jax
import jax.numpy as jnp
from jax import lax
from jax.sharding import PartitionSpec as P


def expand_tiles(values, pattern):
    tile_rows, layers, tile_cols = pattern.shape
    tile_size = values.shape[0] // tile_rows
    blocks = values.reshape(tile_rows, tile_size, layers, tile_cols, tile_size)
    blocks = blocks * pattern[:, None, :, :, None].astype(values.dtype)
    return blocks.reshape(values.shape)


def per_device(left_values, left_pattern, right_values, right_pattern):
    left_block = expand_tiles(left_values, left_pattern)
    right_block = expand_tiles(right_values, right_pattern)
    rows_local = left_block.shape[0]
    columns_local = left_block.shape[2]
    left_flat = left_block.reshape(rows_local, columns_local)
    right_flat = right_block.reshape(right_block.shape[0], -1)
    right_all = lax.all_gather(right_flat, "row", axis=0, tiled=True)
    left_all = lax.all_gather(left_flat, "col", axis=1, tiled=True)
    partial = jnp.dot(left_all, right_all, preferred_element_type=jnp.float32)
    layers = lax.axis_size("layer")
    partial = jnp.stack(
        [partial[:, columns_local * l : columns_local * (l + 1)] for l in range(layers)], axis=0
    )
    product = lax.psum_scatter(partial, "layer", scatter_dimension=0, tiled=True)
    product = product.reshape(rows_local, 1, columns_local)
    squared = product * product
    column = lax.psum(jnp.sum(squared, axis=0, keepdims=True), "row")
    rows_total = rows_local * lax.axis_size("row")
    colmean = column / rows_total
    return (squared / (colmean + 1e-06)).astype(jnp.bfloat16)


def solution(mesh):
    return jax.shard_map(
        per_device,
        mesh=mesh,
        in_specs=(
            P("row", "layer", "col"),
            P("row", "layer", "col"),
            P(("layer", "row"), None, "col"),
            P(("layer", "row"), None, "col"),
        ),
        out_specs=P("row", "layer", "col"),
        check_vma=False,
    )
```

profile of v0, /device:TPU:32, one launch (start us, length us, event | category | flops | bytes accessed | tf_op | source)
XLA Modules:
  0.0 194.0 jit_solution(14705510479955236059)
XLA Ops:
  6.5 0.0 all-gather.3.cloned.1.call-start
  6.5 0.7 convert_bitcast_fusion.1
  7.2 0.1 broadcast_bitcast_fusion
  7.3 2.0 %bitcast_multiply_fusion = bf16[1024,256]{1,0:T(8,128)(2,1)} fusion(bf16[1024,1,256]{2,0,1:T(8,128)(2,1)} %param.4, bf16[1024]{0:T(1024)(128)(2,1)S(1)} %bitcast.29), kind=kLoop, calls=%fused_computation.8 | loop fusion | flops 262144 | bytes 1050624 | tf_op jit(solution)/shard_map/mul | solution.py:11
  9.3 0.0 all-gather.3.cloned.1.call-update
  9.3 0.0 all-gather.5.cloned.1.call-start
  9.4 0.7 convert_bitcast_fusion
  10.1 1.3 broadcast_multiply_fusion
  11.4 0.9 copy.6
  12.3 0.0 all-gather.5.cloned.1.call-update
  12.4 0.0 reduce-scatter.2.cloned.1.call-start
  12.4 62.3 %all-gather.3.cloned.1.call-done = bf16[1024,2048]{1,0:T(8,128)(2,1)} async-done(((bf16[1024,256]{1,0:T(8,128)(2,1)}), bf16[1024,2048]{1,0:T(8,128)(2,1)}) %all-gather.3.cloned.1.call-update) | async-done | bytes 4194320 | tf_op jit(solution)/shard_map/all_gather | solution.py:23
  74.7 35.0 %all-gather.5.cloned.1.call-done = bf16[2048,1024]{1,0:T(8,128)(2,1)} async-done(((bf16[256,1024]{1,0:T(8,128)(2,1)}), bf16[2048,1024]{1,0:T(8,128)(2,1)}) %all-gather.5.cloned.1.call-update) | async-done | bytes 4194320 | tf_op jit(solution)/shard_map/all_gather | solution.py:22
  109.7 7.5 %fusion.1 = f32[1024,1024]{1,0:T(8,128)S(1)} fusion(bf16[1024,2048]{1,0:T(8,128)(2,1)} %all-gather.3.cloned.1.call-done, bf16[2048,1024]{1,0:T(8,128)(2,1)} %all-gather.5.cloned.1.call-done), kind=kOutput, calls=%fused_computation.14 | convolution fusion | flops 4294967296 | bytes 12582912 | tf_op jit(solution)/shard_map/dot_general | solution.py:24
  117.2 0.4 slice_bitcast_fusion.3
  117.6 2.2 %pad_maximum_fusion = f32[4,1024,256]{2,1,0:T(8,128)} fusion(f32[1,1024,256]{2,1,0:T(8,128)S(1)} %get-tuple-element.6, f32[1,1024,256]{2,1,0:T(8,128)S(1)} %get-tuple-element.7, f32[1,1024,256]{2,1,0:T(8,128)S(1)} %get-tuple-element.8, f32[1,1024,256]{2,1,0:T(8,128)S(1)} %get-tuple-element.5), kind=kLoop, calls=%fused_computation | loop fusion | flops 3145728 | bytes 8388608 | tf_op jit(solution)/shard_map/stack | solution.py:26
  119.8 0.0 reduce-scatter.2.cloned.1.call-update
  119.8 49.5 %reduce-scatter.2.cloned.1.call-done = f32[1,1024,256]{2,1,0:T(8,128)} async-done(((f32[4,1024,256]{2,1,0:T(8,128)}), f32[1,1024,256]{2,1,0:T(8,128)}) %reduce-scatter.2.cloned.1.call-update) | async-done | bytes 1048592 | tf_op jit(solution)/shard_map/reduce_scatter | solution.py:29
  169.3 1.4 multiply_reduce_fusion
  170.7 14.6 %psum.7 = f32[1,1,256]{2,1,0:T(1,128)S(1)} all-reduce(f32[1,1,256]{2,1,0:T(1,128)S(1)} %bitcast.30), channel_id=1, replica_groups=mesh['layer'=4,'row'=8,'col'=8] {'row'}, use_global_device_ids=true, to_apply=%region_2.0 | all-reduce | flops 256 | bytes 2048 | tf_op jit(solution)/shard_map/psum | solution.py:32
  185.3 2.1 %fusion = bf16[1024,1,256]{2,0,1:T(8,128)(2,1)} fusion(f32[1,1024,256]{2,1,0:T(8,128)} %reduce-scatter.2.cloned.1.call-done, f32[256]{0:T(256)S(1)} %bitcast.31), kind=kLoop, calls=%fused_computation.6 | loop fusion | flops 786432 | bytes 1573888 | tf_op jit(solution)/shard_map/convert_element_type | solution.py:35
  (2 shorter events, 0.0 us)
Async XLA Ops:
  6.5 68.1 %all-gather.3.cloned.1.call-start = ((), (), s32[]{:S(2)}) async-start(), calls=%async_computation.1 | async-start | bytes 4718592 | tf_op jit(solution)/shard_map/all_gather | solution.py:23
  9.3 100.4 %all-gather.5.cloned.1.call-start = ((), (), s32[]{:S(2)}) async-start(), calls=%async_computation.2 | async-start | bytes 4718592 | tf_op jit(solution)/shard_map/all_gather | solution.py:22
  12.4 156.9 %reduce-scatter.2.cloned.1.call-start = ((), (), s32[]{:S(2)}) async-start(), calls=%async_computation.3 | async-start | bytes 5242880 | tf_op jit(solution)/shard_map/reduce_scatter | solution.py:29
Sparse Core Ops, SparseCore 0:
  9.5 65.1 all-gather.2
  76.5 33.1 all-gather.4
  120.0 49.2 reduce-scatter.1
where the time goes:
time: 194 us
  waiting for transfers between devices  147 us (76%)
  blocking collectives  14.6 us (8%)
  between operations  13.1 us (7%)
  other arithmetic  10.4 us (5%)
  matrix products  7.5 us (4%)
    all_gather x1, waiting for transfers between devices, per_device(): left_all = lax.all_gather(left_flat, 'col', axis=1, tiled=True)  62.3 us
    reduce_scatter x1, waiting for transfers between devices, per_device(): lax.psum_scatter(partial, 'layer', scatter_dimension=0, tiled=True)  49.5 us
    all_gather x1, waiting for transfers between devices, per_device(): right_all = lax.all_gather(right_flat, 'row', axis=0, tiled=True)  35 us
    psum x1, blocking collectives, per_device(): column = lax.psum(jnp.sum(squared, axis=0, keepdims=True), 'row')  14.6 us
    dot_general x1, matrix products, per_device(): partial = jnp.dot(left_all, right_all, preferred_element_type=jnp.float32)  7.5 us
  transfers between devices with their start and end apart: 3, of which 3 were waited for; matrix products, arithmetic and copies ran while one was open for 2% of the time, Pallas kernels for 0%

commit v1 on v0

--- a/solution.py
+++ b/solution.py
@@ -20,7 +20,9 @@
     left_flat = left_block.reshape(rows_local, columns_local)
     right_flat = right_block.reshape(right_block.shape[0], -1)
     right_all = lax.all_gather(right_flat, "row", axis=0, tiled=True)
-    left_all = lax.all_gather(left_flat, "col", axis=1, tiled=True)
+    left_all = jnp.concatenate(
+        lax.all_to_all(jnp.stack([left_flat] * lax.axis_size("col")), "col", 0, 0), axis=1
+    )
     partial = jnp.dot(left_all, right_all, preferred_element_type=jnp.float32)
     layers = lax.axis_size("layer")
     partial = jnp.stack(

time: 194 us -> 197 us (1.015)
  starting transfers between devices: 0.09 us -> 8.74 us
  waiting for transfers between devices: 147 us -> 140 us
  local copies, waits for them, and re-layouts: 1.42 us -> 4.07 us
  other arithmetic: 10.4 us -> 7.91 us
    all_to_all x0 -> x1, waiting for transfers between devices: none -> 93.5 us  [per_device(): lax.all_to_all(jnp.stack([left_flat] * lax.axis_size('col')), 'col', 0, 0)]
    all_gather x1 -> x0, waiting for transfers between devices: 62.3 us -> none  [per_device(): left_all = lax.all_gather(left_flat, 'col', axis=1, tiled=True)]
    all_gather x1, waiting for transfers between devices: 35 us -> 0.01 us  [per_device(): right_all = lax.all_gather(right_flat, 'row', axis=0, tiled=True)]
    all_to_all x0 -> x1, starting transfers between devices: none -> 8.7 us  [per_device(): lax.all_to_all(jnp.stack([left_flat] * lax.axis_size('col')), 'col', 0, 0)]
    another operation x0 -> x1, local copies, waits for them, and re-layouts: none -> 2.49 us  [per_device(): jnp.stack([left_flat] * lax.axis_size('col'))]
    reduce_scatter x1, waiting for transfers between devices: 49.5 us -> 47 us  [per_device(): lax.psum_scatter(partial, 'layer', scatter_dimension=0, tiled=True)]
  transfers between devices with their start and end apart: 3 -> 3, of which waited for: 3 -> 2; matrix products, arithmetic and copies ran while one was open for 2% -> 1% of each run, Pallas kernels for 0% -> 0%
where the time goes in v1:
time: 197 us
  waiting for transfers between devices  140 us (71%)
  blocking collectives  14.6 us (7%)
  between operations  13.5 us (7%)
  starting transfers between devices  8.74 us (4%)
  other arithmetic  7.91 us (4%)
  matrix products  7.58 us (4%)
  local copies, waits for them, and re-layouts  4.07 us (2%)
    all_to_all x1, waiting for transfers between devices, per_device(): lax.all_to_all(jnp.stack([left_flat] * lax.axis_size('col')), 'col', 0, 0)  93.5 us
    reduce_scatter x1, waiting for transfers between devices, per_device(): lax.psum_scatter(partial, 'layer', scatter_dimension=0, tiled=True)  47 us
    psum x1, blocking collectives, per_device(): column = lax.psum(jnp.sum(squared, axis=0, keepdims=True), 'row')  14.6 us
    all_to_all x1, starting transfers between devices, per_device(): lax.all_to_all(jnp.stack([left_flat] * lax.axis_size('col')), 'col', 0, 0)  8.7 us
    dot_general x1, matrix products, per_device(): partial = jnp.dot(left_all, right_all, preferred_element_type=jnp.float32)  7.58 us
  transfers between devices with their start and end apart: 3, of which 2 were waited for; matrix products, arithmetic and copies ran while one was open for 1% of the time, Pallas kernels for 0%

profile of v1, /device:TPU:32, one launch (start us, length us, event | category | flops | bytes accessed | tf_op | source)
XLA Modules:
  0.0 196.9 jit_solution(403520385049782168)
XLA Ops:
  6.5 0.7 convert_bitcast_fusion.1
  7.2 0.1 broadcast_bitcast_fusion
  7.3 1.2 bitcast_multiply_fusion
  8.5 0.2 copy.5
  8.7 2.5 %stack.18 = bf16[8,1024,256]{1,2,0:T(8,128)(2,1)} broadcast(bf16[1024,256]{0,1:T(8,128)(2,1)S(1)} %copy.5), dimensions={1,2} | broadcast | bytes 4718592 | tf_op jit(solution)/shard_map/stack | solution.py:24
  11.2 0.0 copy-start.1
  11.2 0.0 copy-start
  11.2 8.7 %all-to-all-start = ((bf16[8,1024,256]{1,2,0:T(8,128)(2,1)}), bf16[8,1024,256]{1,2,0:T(8,128)(2,1)}, u32[]{:S(2)}, u32[]{:S(2)}) async-start(bf16[8,1024,256]{1,2,0:T(8,128)(2,1)} %stack.18), calls=%async_computation | async-start | bytes 8388608 | tf_op jit(solution)/shard_map/all_to_all | solution.py:24
  19.9 0.0 all-gather.2.cloned.1.call-start
  19.9 0.0 copy-done.1
  20.0 0.0 copy-done
  20.0 0.3 broadcast_multiply_fusion
  20.3 0.9 copy.7
  21.1 0.0 all-gather.2.cloned.1.call-update
  21.2 0.0 reduce-scatter.2.cloned.1.call-start
  21.2 93.5 %all-to-all-done = bf16[8,1024,256]{1,2,0:T(8,128)(2,1)} async-done(((bf16[8,1024,256]{1,2,0:T(8,128)(2,1)}), bf16[8,1024,256]{1,2,0:T(8,128)(2,1)}, u32[]{:S(2)}, u32[]{:S(2)}) %all-to-all-start) | async-done | bytes 4194336 | tf_op jit(solution)/shard_map/all_to_all | solution.py:24
  114.7 7.6 %fusion.1 = f32[1024,1024]{1,0:T(8,128)S(1)} fusion(bf16[1024,2048]{0,1:T(8,128)(2,1)} %bitcast.3, bf16[2048,1024]{1,0:T(8,128)(2,1)} %all-gather.2.cloned.1.call-done), kind=kOutput, calls=%fused_computation.14 | convolution fusion | flops 4294967296 | bytes 12582912 | tf_op jit(solution)/shard_map/dot_general | solution.py:26
  122.3 0.4 slice_bitcast_fusion.3
  122.7 2.2 %pad_maximum_fusion = f32[4,1024,256]{2,1,0:T(8,128)} fusion(f32[1,1024,256]{2,1,0:T(8,128)S(1)} %get-tuple-element.6, f32[1,1024,256]{2,1,0:T(8,128)S(1)} %get-tuple-element.7, f32[1,1024,256]{2,1,0:T(8,128)S(1)} %get-tuple-element.8, f32[1,1024,256]{2,1,0:T(8,128)S(1)} %get-tuple-element.5), kind=kLoop, calls=%fused_computation | loop fusion | flops 3145728 | bytes 8388608 | tf_op jit(solution)/shard_map/stack | solution.py:28
  124.9 0.0 reduce-scatter.2.cloned.1.call-update
  124.9 47.0 %reduce-scatter.2.cloned.1.call-done = f32[1,1024,256]{2,1,0:T(8,128)} async-done(((f32[4,1024,256]{2,1,0:T(8,128)}), f32[1,1024,256]{2,1,0:T(8,128)}) %reduce-scatter.2.cloned.1.call-update) | async-done | bytes 1048592 | tf_op jit(solution)/shard_map/reduce_scatter | solution.py:31
  171.9 1.4 multiply_reduce_fusion
  173.3 14.6 %psum.7 = f32[1,1,256]{2,1,0:T(1,128)S(1)} all-reduce(f32[1,1,256]{2,1,0:T(1,128)S(1)} %bitcast.33), channel_id=1, replica_groups=mesh['layer'=4,'row'=8,'col'=8] {'row'}, use_global_device_ids=true, to_apply=%region_2.0 | all-reduce | flops 256 | bytes 2048 | tf_op jit(solution)/shard_map/psum | solution.py:34
  187.9 2.1 %fusion = bf16[1024,1,256]{2,0,1:T(8,128)(2,1)} fusion(f32[1,1024,256]{2,1,0:T(8,128)} %reduce-scatter.2.cloned.1.call-done, f32[256]{0:T(256)S(1)} %bitcast.34), kind=kLoop, calls=%fused_computation.6 | loop fusion | flops 786432 | bytes 1573888 | tf_op jit(solution)/shard_map/convert_element_type | solution.py:37
  (4 shorter events, 0.0 us)
Async XLA Ops:
  11.2 8.7 %copy-start.1 = (s32[1,4,1]{1,2,0:T(1,128)S(1)}, s32[1,4,1]{1,2,0:T(1,128)}, u32[]{:S(2)}) copy-start(s32[1,4,1]{1,2,0:T(1,128)} %param.7) | copy-start | bytes 52
  11.2 8.7 %copy-start = (bf16[256,4,256]{2,1,0:T(4,128)(2,1)S(1)}, bf16[256,4,256]{2,1,0:T(4,128)(2,1)}, u32[]{:S(2)}) copy-start(bf16[256,4,256]{2,1,0:T(4,128)(2,1)} %param.6) | copy-start | bytes 1572868
  11.2 103.5 %all-to-all-start = ((bf16[8,1024,256]{1,2,0:T(8,128)(2,1)}), bf16[8,1024,256]{1,2,0:T(8,128)(2,1)}, u32[]{:S(2)}, u32[]{:S(2)}) async-start(bf16[8,1024,256]{1,2,0:T(8,128)(2,1)} %stack.18), calls=%async_computation | async-start | bytes 8388608 | tf_op jit(solution)/shard_map/all_to_all | solution.py:24
  19.9 94.8 %all-gather.2.cloned.1.call-start = ((), (), s32[]{:S(2)}) async-start(), calls=%async_computation.2 | async-start | bytes 4718592 | tf_op jit(solution)/shard_map/all_gather | solution.py:22
  21.2 150.7 %reduce-scatter.2.cloned.1.call-start = ((), (), s32[]{:S(2)}) async-start(), calls=%async_computation.3 | async-start | bytes 5242880 | tf_op jit(solution)/shard_map/reduce_scatter | solution.py:31
Sparse Core Ops, SparseCore 0:
  22.6 35.9 all-gather.1
  125.1 46.7 reduce-scatter.1

commit v2 on v0

--- a/solution.py
+++ b/solution.py
@@ -2,6 +2,14 @@
 import jax.numpy as jnp
 from jax import lax
 from jax.sharding import PartitionSpec as P
+
+
+def gather_by_exchange(value, axis, dim):
+    devices = lax.axis_size(axis)
+    repeats = [devices if d == dim else 1 for d in range(value.ndim)]
+    return lax.all_to_all(
+        jnp.tile(value, repeats), axis, split_axis=dim, concat_axis=dim, tiled=True
+    )
 
 
 def expand_tiles(values, pattern):
@@ -19,7 +27,7 @@
     columns_local = left_block.shape[2]
     left_flat = left_block.reshape(rows_local, columns_local)
     right_flat = right_block.reshape(right_block.shape[0], -1)
-    right_all = lax.all_gather(right_flat, "row", axis=0, tiled=True)
+    right_all = gather_by_exchange(right_flat, "row", 0)
     left_all = lax.all_gather(left_flat, "col", axis=1, tiled=True)
     partial = jnp.dot(left_all, right_all, preferred_element_type=jnp.float32)
     layers = lax.axis_size("layer")

time: 194 us -> 158 us (0.81)
  waiting for transfers between devices: 147 us -> 55.9 us
  blocking collectives: 14.6 us -> 69.4 us
    all_to_all x0 -> x1, blocking collectives: none -> 54.7 us  [gather_by_exchange(): lax.all_to_all(jnp.tile(value, repeats), axis, split_axis=dim, concat_axi...]
    all_gather x1, waiting for transfers between devices: 62.3 us -> 7.55 us  [per_device(): left_all = lax.all_gather(left_flat, 'col', axis=1, tiled=True)]
    all_gather x1 -> x0, waiting for transfers between devices: 35 us -> none  [per_device(): right_all = lax.all_gather(right_flat, 'row', axis=0, tiled=True)]
  transfers between devices with their start and end apart: 3 -> 2, of which waited for: 3 -> 2; matrix products, arithmetic and copies ran while one was open for 2% -> 2% of each run, Pallas kernels for 0% -> 0%
where the time goes in v2:
time: 158 us
  blocking collectives  69.4 us (44%)
  waiting for transfers between devices  55.9 us (35%)
  between operations  13.4 us (8%)
  other arithmetic  10.4 us (7%)
  matrix products  7.5 us (5%)
    all_to_all x1, blocking collectives, gather_by_exchange(): lax.all_to_all(jnp.tile(value, repeats), axis, split_axis=dim, concat_axi...  54.7 us
    reduce_scatter x1, waiting for transfers between devices, per_device(): lax.psum_scatter(partial, 'layer', scatter_dimension=0, tiled=True)  48.3 us
    psum x1, blocking collectives, per_device(): column = lax.psum(jnp.sum(squared, axis=0, keepdims=True), 'row')  14.7 us
    all_gather x1, waiting for transfers between devices, per_device(): left_all = lax.all_gather(left_flat, 'col', axis=1, tiled=True)  7.55 us
    dot_general x1, matrix products, per_device(): partial = jnp.dot(left_all, right_all, preferred_element_type=jnp.float32)  7.5 us
    mul x2, other arithmetic, expand_tiles(): blocks = blocks * pattern[:, None, :, :, None].astype(values.dtype)  3.37 us
  transfers between devices with their start and end apart: 2, of which 2 were waited for; matrix products, arithmetic and copies ran while one was open for 2% of the time, Pallas kernels for 0%

profile of v2, /device:TPU:32, one launch (start us, length us, event | category | flops | bytes accessed | tf_op | source)
XLA Modules:
  0.0 157.7 jit_solution(4230839220704612140)
XLA Ops:
  6.5 0.0 all-gather.2.cloned.1.call-start
  6.5 0.7 convert_bitcast_fusion.1
  7.2 0.1 broadcast_bitcast_fusion
  7.3 2.0 %bitcast_multiply_fusion = bf16[1024,256]{1,0:T(8,128)(2,1)} fusion(bf16[1024,1,256]{2,0,1:T(8,128)(2,1)} %param.4, bf16[1024]{0:T(1024)(128)(2,1)S(1)} %bitcast.31), kind=kLoop, calls=%fused_computation.8 | loop fusion | flops 262144 | bytes 1050624 | tf_op jit(solution)/shard_map/mul | solution.py:19
  9.3 0.0 all-gather.2.cloned.1.call-update
  9.3 0.0 reduce-scatter.2.cloned.1.call-start
  9.4 0.7 convert_bitcast_fusion
  10.1 1.3 broadcast_multiply_fusion
  11.4 0.1 copy.6
  11.5 0.5 tile.9
  12.0 54.7 %all_to_all.9 = bf16[8,256,1024]{2,1,0:T(8,128)(2,1)} all-to-all(bf16[8,256,1024]{2,1,0:T(8,128)(2,1)S(1)} %tile.9), channel_id=1, replica_groups=mesh['layer'=4,'row'=8,'col'=8] {'row'}, dimensions={0} | all-to-all | bytes 8388608 | tf_op jit(solution)/shard_map/all_to_all | solution.py:10
  66.7 7.6 %all-gather.2.cloned.1.call-done = bf16[1024,2048]{1,0:T(8,128)(2,1)} async-done(((bf16[1024,256]{1,0:T(8,128)(2,1)}), bf16[1024,2048]{1,0:T(8,128)(2,1)}) %all-gather.2.cloned.1.call-update) | async-done | bytes 4194320 | tf_op jit(solution)/shard_map/all_gather | solution.py:31
  74.3 7.5 %fusion.1 = f32[1024,1024]{1,0:T(8,128)S(1)} fusion(bf16[1024,2048]{1,0:T(8,128)(2,1)} %all-gather.2.cloned.1.call-done, bf16[2048,1024]{1,0:T(8,128)(2,1)} %bitcast.28), kind=kOutput, calls=%fused_computation.14 | convolution fusion | flops 4294967296 | bytes 12582912 | tf_op jit(solution)/shard_map/dot_general | solution.py:32
  81.8 0.4 slice_bitcast_fusion.3
  82.2 2.2 %pad_maximum_fusion = f32[4,1024,256]{2,1,0:T(8,128)} fusion(f32[1,1024,256]{2,1,0:T(8,128)S(1)} %get-tuple-element.6, f32[1,1024,256]{2,1,0:T(8,128)S(1)} %get-tuple-element.7, f32[1,1024,256]{2,1,0:T(8,128)S(1)} %get-tuple-element.8, f32[1,1024,256]{2,1,0:T(8,128)S(1)} %get-tuple-element.5), kind=kLoop, calls=%fused_computation | loop fusion | flops 3145728 | bytes 8388608 | tf_op jit(solution)/shard_map/stack | solution.py:34
  84.4 0.0 reduce-scatter.2.cloned.1.call-update
  84.4 48.3 %reduce-scatter.2.cloned.1.call-done = f32[1,1024,256]{2,1,0:T(8,128)} async-done(((f32[4,1024,256]{2,1,0:T(8,128)}), f32[1,1024,256]{2,1,0:T(8,128)}) %reduce-scatter.2.cloned.1.call-update) | async-done | bytes 1048592 | tf_op jit(solution)/shard_map/reduce_scatter | solution.py:37
  132.7 1.4 multiply_reduce_fusion
  134.1 14.7 %psum.7 = f32[1,1,256]{2,1,0:T(1,128)S(1)} all-reduce(f32[1,1,256]{2,1,0:T(1,128)S(1)} %bitcast.32), channel_id=1, replica_groups=mesh['layer'=4,'row'=8,'col'=8] {'row'}, use_global_device_ids=true, to_apply=%region_2.0 | all-reduce | flops 256 | bytes 2048 | tf_op jit(solution)/shard_map/psum | solution.py:40
  148.8 2.1 %fusion = bf16[1024,1,256]{2,0,1:T(8,128)(2,1)} fusion(f32[1,1024,256]{2,1,0:T(8,128)} %reduce-scatter.2.cloned.1.call-done, f32[256]{0:T(256)S(1)} %bitcast.33), kind=kLoop, calls=%fused_computation.6 | loop fusion | flops 786432 | bytes 1573888 | tf_op jit(solution)/shard_map/convert_element_type | solution.py:43
  (2 shorter events, 0.0 us)
Async XLA Ops:
  6.5 67.7 %all-gather.2.cloned.1.call-start = ((), (), s32[]{:S(2)}) async-start(), calls=%async_computation.2 | async-start | bytes 4718592 | tf_op jit(solution)/shard_map/all_gather | solution.py:31
  9.3 123.4 %reduce-scatter.2.cloned.1.call-start = ((), (), s32[]{:S(2)}) async-start(), calls=%async_computation.3 | async-start | bytes 5242880 | tf_op jit(solution)/shard_map/reduce_scatter | solution.py:37
Sparse Core Ops, SparseCore 0:
  9.5 64.7 all-gather.1
  84.5 48.1 reduce-scatter.1
